TPU v7x, 256 devices: a whole 4x4x8 slice. The times are simulated.
256 devices in a mesh: blk: 32 (over y, x, core), line: 8 (over z).
Axes of the slice: x: 4, y: 4, z: 8, core: 2. Of those that a mesh axis runs over, the one named last changes fastest.
Arguments:
- state: float32 [128, 5, 64, 4096], P('blk', None, 'line'), may hold values from -6 to 6
- viscous: float32 [128, 3, 5], P('blk'), may hold values from 0.1 to 1
- advection: float32 [128, 3, 5], P('blk'), may hold values from -1 to 1
- sweep_inverse: float32 [128, 3, 5, 64, 64], P('blk'), as said below
- face_links: int32 [128, 4, 3], P('blk'), may hold values from -1 to 127, as said below
Outputs:
- update: float32 [128, 5, 64, 4096], P('blk', None, None, 'line')
Inputs may be any that keep to these rules, and one draw needn't show every extreme that they name: `face_links`: links are mutual: if face f of block b names (c, g, o) then face g of block c names (b, f, o). A wall face holds -1, 0, 0. No face names a block of its own blk index. For every blk index there is another index whose blocks are named by exactly 2 of its faces, and no pair of indices has more. `sweep_inverse`: per block, direction and field a full 64 x 64 matrix.
All inputs are finite; a program needn't handle non-finite values.
Results may differ from a plain program's by a relative error of at most 0.000071.
Values sent between devices are 32-bit elements; how exact they have to be, the bound alone decides.
A program may use at most 192 MiB of HBM per device.

v0:
```python
import functools

import jax
import jax.numpy as jnp
from jax import lax
from jax.experimental import pallas as pl
from jax.experimental.pallas import tpu as pltpu
from jax.sharding import PartitionSpec as P

MESH = pl.DeviceIdType.MESH
F32 = jnp.float32
BF16 = jnp.bfloat16

NB = 4
NF = 5
NU = NB * NF
NL = 64
ROWS = 8
PAIRS = 32
FACES = 4 * NB
CODES = 128


def link_codes(face_links, blocks_here, count):
    rows = face_links.reshape(FACES, 3)
    neighbor, face, flip = rows[:, 0], rows[:, 1], rows[:, 2]
    linked = neighbor >= 0
    peer = jnp.where(linked, neighbor // blocks_here, -1)
    their = jnp.where(linked, (neighbor % blocks_here) * 4 + face, 0)
    number = jnp.arange(FACES, dtype=jnp.int32)
    same = (peer[:, None] == peer[None, :]) & linked[:, None]
    rank = jnp.sum(same & (number[None, :] < number[:, None]), axis=1)
    place = jnp.sum(same & (their[None, :] < their[:, None]), axis=1)
    target = jnp.arange(2 * count, dtype=jnp.int32)
    hit = (peer[None, :] == target[:, None] // 2) & (rank[None, :] == target[:, None] % 2)
    sent = jnp.sum(jnp.where(hit, 2 * number + flip, 0), axis=1)
    source = jnp.where(linked, peer, 0)
    slot = jnp.where(linked, place, 2)
    tail = jnp.zeros((CODES - 2 * count - 2 * FACES,), jnp.int32)
    return jnp.concatenate([sent, source, slot, tail]).astype(jnp.int32)


def split(value):
    high = value.astype(BF16)
    low = (value - high.astype(F32)).astype(BF16)
    return high, low


def kernel(
    blks, lines,
    codes, viscous, advection, state, inverse, out,
    points, inv, weight_k, weight_j, weight_i, own, table, slots, arrived,
    rim_out, rim_in, halo_j, halo_k, turned, sent, lines_in, result,
    load_sem, inv_sem, rim_send, rim_recv, face_send, face_recv, line_send, line_recv, out_sem,
):
    me = lax.axis_index("blk")
    row = lax.axis_index("line")

    def load(pair):
        return pltpu.make_async_copy(
            state.at[:, :, pl.ds(pair * 128, 128)],
            points.at[:, pl.ds(pair * ROWS, ROWS), :],
            load_sem,
        )

    for pair in range(PAIRS):
        load(pair).start()
    inv_copy = pltpu.make_async_copy(inverse, inv, inv_sem)
    inv_copy.start()

    barrier = pltpu.get_barrier_semaphore()

    def greet_blk(step, carry):
        pl.semaphore_signal(
            barrier, inc=1, device_id=(lax.rem(me + step, blks), row), device_id_type=MESH
        )
        return carry

    def greet_line(step, carry):
        pl.semaphore_signal(
            barrier, inc=1, device_id=(me, lax.rem(row + step, lines)), device_id_type=MESH
        )
        return carry

    lax.fori_loop(1, blks, greet_blk, 0)
    lax.fori_loop(1, lines, greet_line, 0)

    lane = lax.broadcasted_iota(jnp.int32, (ROWS, 128), 1)
    level = lax.broadcasted_iota(jnp.int32, (ROWS, 128), 0)
    left = lane < 64
    even = (lane & 1) == 0

    pltpu.make_async_copy(points, points, load_sem).wait()

    def take_rims(unit, carry):
        rim_out[0, unit] = points[unit, pl.ds(0, PAIRS, stride=ROWS), :]
        rim_out[1, unit] = points[unit, pl.ds(ROWS - 1, PAIRS, stride=ROWS), :]
        return carry

    lax.fori_loop(0, NU, take_rims, 0)

    def merged(values):
        count = 1
        shift = (lane + 1) & 63
        while values.shape[0] > 1:
            pairs = values.reshape(values.shape[0] // 2, 2, ROWS, 128)
            moved = pltpu.roll(pairs[:, 1], 2 * count, axis=2)
            values = jnp.where((shift < 2 * count)[None], pairs[:, 0], moved)
            count *= 2
        return values[0]

    def take_faces(unit, carry):
        block, field = unit // NF, lax.rem(unit, NF)
        cells = points[unit].reshape(PAIRS, ROWS, 128)
        own[2 * block, field] = jnp.where(left, cells[0], cells[PAIRS - 1])
        mixed = merged(cells)
        low = jnp.where(even, mixed, pltpu.roll(mixed, 65, axis=1))
        high = jnp.where(even, pltpu.roll(mixed, 1, axis=1), pltpu.roll(mixed, 66, axis=1))
        own[2 * block + 1, field] = jnp.where(left, low, high)
        return carry

    lax.fori_loop(0, NU, take_faces, 0)

    def fill_table(item, carry):
        pair, field = item // NF, lax.rem(item, NF)
        forward = own[pair, field]
        backward = forward
        for bit in (1, 2, 4, 8, 16, 32):
            backward = jnp.where(
                (lane & bit) != 0,
                pltpu.roll(backward, bit, axis=1),
                pltpu.roll(backward, 128 - bit, axis=1),
            )
        for flip, value in ((0, forward), (1, backward)):
            other = pltpu.roll(value, 64, axis=1)
            table[4 * pair + flip, field] = jnp.where(left, value, other)
            table[4 * pair + 2 + flip, field] = jnp.where(left, other, value)
        return carry

    lax.fori_loop(0, 2 * NB * NF, fill_table, 0)

    pl.semaphore_wait(barrier, blks + lines - 2)

    rims = [
        pltpu.make_async_remote_copy(
            src_ref=rim_out.at[side],
            dst_ref=rim_in.at[1 - side],
            send_sem=rim_send.at[side],
            recv_sem=rim_recv.at[1 - side],
            device_id=(me, lax.rem(row + (lines - 1 if side == 0 else 1), lines)),
            device_id_type=MESH,
        )
        for side in (0, 1)
    ]
    for rim in rims:
        rim.start()

    def send_faces(step, carry):
        target = lax.rem(me + step, blks)
        slots[target] = jnp.where(
            left[None], table[codes[2 * target]], table[codes[2 * target + 1]]
        )
        pltpu.make_async_remote_copy(
            src_ref=slots.at[target],
            dst_ref=arrived.at[me],
            send_sem=face_send,
            recv_sem=face_recv,
            device_id=(target, row),
            device_id_type=MESH,
        ).start()
        return carry

    lax.fori_loop(1, blks, send_faces, 0)

    inv_copy.wait()
    deep = lax.broadcasted_iota(jnp.int32, (NL, 128), 0)
    wide = lax.broadcasted_iota(jnp.int32, (NL, 128), 1)
    ones = jnp.ones((NL, 128), F32)
    zeros = jnp.zeros((NL, 128), F32)
    at_left = jnp.where(deep == wide, ones, zeros).astype(BF16)
    at_right = jnp.where(deep + NL == wide, ones, zeros).astype(BF16)
    column = wide & 63
    order = 2 * (column & 31) + (column >> 5)
    picked = jnp.where(deep == order, ones, zeros)
    pick_left = jnp.where(wide < 64, picked, zeros).astype(BF16)
    pick_right = jnp.where(wide < 64, zeros, picked).astype(BF16)

    def place(value, where):
        return jnp.dot(value, where, preferred_element_type=F32)

    def make_weights(unit, carry):
        block, field = unit // NF, lax.rem(unit, NF)
        base = block * 3 * NF + field
        high, low = split(inv[base + 2 * NF])
        weight_k[unit, 0:64] = place(high, at_left).astype(BF16)
        weight_k[unit, 64:128] = place(high, at_right).astype(BF16)
        weight_k[unit, 128:192] = place(low, at_left).astype(BF16)
        weight_k[unit, 192:256] = place(low, at_right).astype(BF16)
        along_j = jnp.concatenate(
            [
                inv[base + NF, pl.ds(0, PAIRS, stride=2), :],
                inv[base + NF, pl.ds(1, PAIRS, stride=2), :],
            ],
            axis=0,
        )
        high, low = split(along_j)
        weight_j[unit] = (place(high, pick_left) + place(low, pick_right)).astype(BF16)
        high, low = split(inv[base])
        weight_i[unit] = (place(high, at_left) + place(low, at_right)).astype(BF16)
        return carry

    lax.fori_loop(0, NU, make_weights, 0)

    for rim in rims:
        rim.wait()
    pltpu.make_async_copy(
        slots.at[pl.ds(0, blks - 1)], slots.at[pl.ds(0, blks - 1)], face_send
    ).wait()
    pltpu.make_async_copy(
        arrived.at[pl.ds(0, blks - 1)], arrived.at[pl.ds(0, blks - 1)], face_recv
    ).wait()

    whole = (NF, ROWS, 128)

    def facing(face, half):
        source, slot = codes[2 * blks + face], codes[2 * blks + FACES + face]
        value = arrived[source]
        slots_of = jnp.full(whole, slot, jnp.int32)
        value = jnp.where(slots_of == half, value, pltpu.roll(value, 64, axis=2))
        return jnp.where(slots_of == 2, own[face // 2], value)

    for pair in range(2 * NB):
        value = jnp.where(left[None], facing(2 * pair, 0), facing(2 * pair + 1, 1))
        block = pair // 2
        if pair % 2 == 0:
            halo_j[pl.ds(block * NF, NF)] = value
        else:
            far = jnp.where(left[None], value, pltpu.roll(value, 63, axis=2))
            ahead = ((lane >= 63) & (lane < 126))[None]
            near = jnp.where(ahead, pltpu.roll(value, 127, axis=2), pltpu.roll(value, 62, axis=2))
            halo_k[pl.ds(block * NF, NF)] = jnp.where(even[None], far, near)

    first = jnp.full((ROWS, 128), row, jnp.int32) == 0
    last = jnp.full((ROWS, 128), row, jnp.int32) == lines - 1
    top, bottom = level == 0, level == ROWS - 1
    k_low, k_high = (lane & 63) == 0, (lane & 63) == 63
    left_wide = lax.broadcasted_iota(jnp.int32, (PAIRS, 128), 1) < 64

    def line_copy(unit, step):
        target = lax.rem(row + step, lines)
        return pltpu.make_async_remote_copy(
            src_ref=sent.at[unit, pl.ds(target * PAIRS, PAIRS), :],
            dst_ref=lines_in.at[unit, row],
            send_sem=line_send.at[unit],
            recv_sem=line_recv.at[unit],
            device_id=(me, target),
            device_id_type=MESH,
        )

    def sweep_jk(unit, carry):
        block, field = unit // NF, lax.rem(unit, NF)
        ahead, behind = [], []
        middle = jnp.float32(0.0)
        for direction in range(3):
            diffuse = viscous[block, direction, field]
            half_speed = 0.5 * advection[block, direction, field]
            ahead.append(diffuse - half_speed)
            behind.append(diffuse + half_speed)
            middle = middle - 2.0 * diffuse
        j_rows, k_rows = halo_j[unit], halo_k[unit]
        cells = [points[unit, pl.ds(pair * ROWS, ROWS), :] for pair in range(PAIRS)]
        turns = [pltpu.roll(cell, 64, axis=1) for cell in cells]
        summed = []
        for pair in range(PAIRS):
            cell, turn = cells[pair], turns[pair]
            below = jnp.broadcast_to(rim_in[0, unit, pl.ds(pair, 1), :], (ROWS, 128))
            above = jnp.broadcast_to(rim_in[1, unit, pl.ds(pair, 1), :], (ROWS, 128))
            below = jnp.where(first, cell, below)
            above = jnp.where(last, cell, above)
            i_minus = jnp.where(top, below, pltpu.roll(cell, 1, axis=0))
            i_plus = jnp.where(bottom, above, pltpu.roll(cell, ROWS - 1, axis=0))
            j_minus = jnp.where(left, turns[pair - 1] if pair else j_rows, turn)
            j_plus = jnp.where(left, turn, turns[pair + 1] if pair < PAIRS - 1 else j_rows)
            edge = pltpu.roll(k_rows, (128 - 2 * pair) % 128, axis=1) if pair else k_rows
            k_minus = jnp.where(k_low, edge, pltpu.roll(cell, 1, axis=1))
            k_plus = jnp.where(k_high, edge, pltpu.roll(cell, 127, axis=1))
            summed.append(
                middle * cell
                + (ahead[0] * i_plus + behind[0] * i_minus)
                + (ahead[1] * j_plus + behind[1] * j_minus)
                + (ahead[2] * k_plus + behind[2] * k_minus)
            )
        high, low = split(jnp.concatenate(summed, axis=0))
        inverse_k = weight_k[unit]
        both = lax.dot_general(
            jnp.concatenate([high, low], axis=1),
            jnp.concatenate([inverse_k, inverse_k], axis=1),
            (((1,), (1,)), ((), ())),
            preferred_element_type=F32,
        )
        turned[...] = both[:, :128] + both[:, 128:]
        columns = []
        for step in range(0, ROWS, 2):
            one = turned[pl.ds(step, PAIRS, stride=ROWS), :]
            two = turned[pl.ds(step + 1, PAIRS, stride=ROWS), :]
            evens = jnp.where(left_wide, one, pltpu.roll(two, 64, axis=1))
            odds = jnp.where(left_wide, pltpu.roll(one, 64, axis=1), two)
            columns.append(jnp.concatenate([evens, odds], axis=0))
        after = sweep(weight_j[unit], jnp.concatenate(columns, axis=1))
        for step in range(0, ROWS, 2):
            evens = after[:PAIRS, step * 64 : step * 64 + 128]
            odds = after[PAIRS:, step * 64 : step * 64 + 128]
            sent[unit, pl.ds(step, PAIRS, stride=ROWS), :] = jnp.where(
                left_wide, evens, pltpu.roll(odds, 64, axis=1)
            )
            sent[unit, pl.ds(step + 1, PAIRS, stride=ROWS), :] = jnp.where(
                left_wide, pltpu.roll(evens, 64, axis=1), odds
            )
        lines_in[unit, row] = sent[unit, pl.ds(row * PAIRS, PAIRS), :]
        for step in (4, 3, 5, 2, 6, 1, 7):
            line_copy(unit, step).start()
        return carry

    def sweep(weight, value):
        high, low = split(value)
        return jnp.dot(
            jnp.concatenate([weight, weight], axis=1),
            jnp.concatenate([high, high, low, low], axis=0),
            preferred_element_type=F32,
        )

    lax.fori_loop(0, NU, sweep_jk, 0)

    others = pl.ds(0, lines - 1)

    def sweep_i(unit, carry):
        pltpu.make_async_copy(
            lines_in.at[unit, others], lines_in.at[unit, others], line_recv.at[unit]
        ).wait()
        values = lines_in[unit]
        columns = [
            values[:, pair * ROWS : (pair + 1) * ROWS, :].reshape(NL, 128) for pair in range(4)
        ]
        result[unit] = sweep(weight_i[unit], jnp.concatenate(columns, axis=1))
        pltpu.make_async_copy(result.at[unit], out.at[unit], out_sem).start()
        return carry

    lax.fori_loop(0, NU, sweep_i, 0)

    def finish(unit, carry):
        pltpu.make_async_copy(
            lines_in.at[unit, others], lines_in.at[unit, others], line_send.at[unit]
        ).wait()
        return carry

    lax.fori_loop(0, NU, finish, 0)
    pltpu.make_async_copy(result, out, out_sem).wait()


def on_device(state, viscous, advection, sweep_inverse, face_links):
    blks, lines = lax.axis_size("blk"), lax.axis_size("line")
    blocks_here, fields, rows_here, plane = state.shape
    codes = link_codes(face_links, blocks_here, blks)
    smem = pl.BlockSpec(memory_space=pltpu.SMEM)
    anywhere = pl.BlockSpec(memory_space=pl.ANY)
    dma = pltpu.SemaphoreType.DMA
    out = pl.pallas_call(
        functools.partial(kernel, blks, lines),
        out_shape=jax.ShapeDtypeStruct((NU, NL, plane // lines), F32),
        in_specs=[smem, smem, smem, anywhere, anywhere],
        out_specs=anywhere,
        scratch_shapes=[
            pltpu.VMEM((NU, PAIRS * ROWS, 128), F32),
            pltpu.VMEM((3 * NU, NL, NL), F32),
            pltpu.VMEM((NU, 256, 128), BF16),
            pltpu.VMEM((NU, NL, 128), BF16),
            pltpu.VMEM((NU, NL, 128), BF16),
            pltpu.VMEM((2 * NB, NF, ROWS, 128), F32),
            pltpu.VMEM((2 * FACES, NF, ROWS, 128), F32),
            pltpu.VMEM((blks, NF, ROWS, 128), F32),
            pltpu.VMEM((blks, NF, ROWS, 128), F32),
            pltpu.VMEM((2, NU, PAIRS, 128), F32),
            pltpu.VMEM((2, NU, PAIRS, 128), F32),
            pltpu.VMEM((NU, ROWS, 128), F32),
            pltpu.VMEM((NU, ROWS, 128), F32),
            pltpu.VMEM((PAIRS * ROWS, 128), F32),
            pltpu.VMEM((NU, PAIRS * ROWS, 128), F32),
            pltpu.VMEM((NU, lines, PAIRS, 128), F32),
            pltpu.VMEM((NU, NL, plane // lines), F32),
            dma, dma, dma((2,)), dma((2,)), dma, dma, dma((NU,)), dma((NU,)), dma,
        ],
        compiler_params=pltpu.CompilerParams(
            collective_id=0, has_side_effects=True, vmem_limit_bytes=40 * 1024 * 1024
        ),
        name="implicit_update",
    )(
        codes,
        viscous,
        advection,
        state.reshape(NU, rows_here, plane),
        sweep_inverse.reshape(3 * NU, NL, NL),
    )
    return out.reshape(blocks_here, fields, NL, plane // lines)


def solution(mesh):
    in_specs = (
        P("blk", None, "line", None),
        P("blk", None, None),
        P("blk", None, None),
        P("blk", None, None, None, None),
        P("blk", None, None),
    )
    out_specs = P("blk", None, None, "line")
    return jax.shard_map(
        on_device, mesh=mesh, in_specs=in_specs, out_specs=out_specs, check_vma=False
    )
```

profile of v0, /device:TPU:1, one launch (start us, length us, event | category | flops | bytes accessed | tf_op | source)
XLA Modules:
  0.0 112.4 jit_solution(3555626741073382590)
XLA Ops:
  0.0 0.8 reshape.128
  0.8 0.2 convert_reduce_fusion.1
  1.0 0.1 select_reduce_fusion
  1.1 0.1 pad_add_fusion.codes
  1.2 0.7 copy.8.viscous
  1.9 0.7 copy.9.advection
  2.6 0.0 copy-start
  2.6 1.7 %copy-done = f32[4,5,8,4096]{3,2,1,0:T(8,128)S(1)} copy-done((f32[4,5,8,4096]{3,2,1,0:T(8,128)S(1)}, f32[4,5,8,4096]{3,2,1,0:T(8,128)}, u32[]{:S(2)}) %copy-start) | copy-done | bytes 2621464
  4.3 0.0 copy-start.1
  4.3 1.5 %copy-done.1 = f32[4,3,5,64,64]{4,3,2,1,0:T(8,128)S(1)} copy-done((f32[4,3,5,64,64]{4,3,2,1,0:T(8,128)S(1)}, f32[4,3,5,64,64]{4,3,2,1,0:T(8,128)}, u32[]{:S(2)}) %copy-start.1) | copy-done | bytes 983064
  5.9 105.0 %implicit_update.1 = f32[20,64,512]{2,1,0:T(8,128)S(1)} custom-call(s32[128]{0:T(128)S(1)} %pad_add_fusion.codes, f32[4,3,5]{2,1,0:T(4,128)S(1)} %copy.8.viscous, f32[4,3,5]{2,1,0:T(4,128)S(1)} %copy.9.advection, f32[20,8,4096]{2,1,0:T(8,128)S(1)} %bitcast.43, f32[60,64,64]{2,1,0:T(8,128)S(1)} %bitcast.44), custom_call_target="tpu_custom_call" | custom-call | tf_op jit(solution)/shard_map/implicit_update/pallas_call | solution.py:367
  110.9 1.5 %copy.11 = f32[4,5,64,512]{3,2,1,0:T(8,128)} copy(f32[4,5,64,512]{3,2,1,0:T(8,128)S(1)} %bitcast.42) | data formatting | bytes 5242880
  (6 shorter events, 0.0 us)
Async XLA Ops:
  2.6 1.7 %copy-start = (f32[4,5,8,4096]{3,2,1,0:T(8,128)S(1)}, f32[4,5,8,4096]{3,2,1,0:T(8,128)}, u32[]{:S(2)}) copy-start(f32[4,5,8,4096]{3,2,1,0:T(8,128)} %param.5) | copy-start | bytes 7864324
  4.3 1.5 %copy-start.1 = (f32[4,3,5,64,64]{4,3,2,1,0:T(8,128)S(1)}, f32[4,3,5,64,64]{4,3,2,1,0:T(8,128)}, u32[]{:S(2)}) copy-start(f32[4,3,5,64,64]{4,3,2,1,0:T(8,128)} %param.8) | copy-start | bytes 2949124
where the time goes:
time: 113 us; the launch traced here: 112 us
  Pallas kernels  105 us (93%)
  local copies, waits for them, and re-layouts  6.94 us (6%)
    pallas_call x1, Pallas kernels, on_device(): pl.pallas_call(functools.partial(kernel, blks, lines), out_shape=jax.Shap...  105 us
    unnamed x7, local copies, waits for them, and re-layouts  6.17 us

commit v1 on v0

--- a/solution.py
+++ b/solution.py
@@ -21,23 +21,35 @@
 CODES = 128
 
 
-def link_codes(face_links, blocks_here, count):
-    rows = face_links.reshape(FACES, 3)
-    neighbor, face, flip = rows[:, 0], rows[:, 1], rows[:, 2]
-    linked = neighbor >= 0
-    peer = jnp.where(linked, neighbor // blocks_here, -1)
-    their = jnp.where(linked, (neighbor % blocks_here) * 4 + face, 0)
-    number = jnp.arange(FACES, dtype=jnp.int32)
-    same = (peer[:, None] == peer[None, :]) & linked[:, None]
-    rank = jnp.sum(same & (number[None, :] < number[:, None]), axis=1)
-    place = jnp.sum(same & (their[None, :] < their[:, None]), axis=1)
-    target = jnp.arange(2 * count, dtype=jnp.int32)
-    hit = (peer[None, :] == target[:, None] // 2) & (rank[None, :] == target[:, None] % 2)
-    sent = jnp.sum(jnp.where(hit, 2 * number + flip, 0), axis=1)
-    source = jnp.where(linked, peer, 0)
-    slot = jnp.where(linked, place, 2)
-    tail = jnp.zeros((CODES - 2 * count - 2 * FACES,), jnp.int32)
-    return jnp.concatenate([sent, source, slot, tail]).astype(jnp.int32)
+def link_codes(links, blocks_here, blks):
+    lane = lax.broadcasted_iota(jnp.int32, (8, CODES), 1)
+    target, slot = lane >> 1, lane & 1
+    number = lane & (FACES - 1)
+    faces = []
+    for face in range(FACES):
+        neighbor, their, flip = (links[part, face // 4, face % 4] for part in range(3))
+        peer = jnp.where(neighbor >= 0, neighbor // blocks_here, -1)
+        faces.append((peer, lax.rem(neighbor, blocks_here) * 4 + their, flip))
+    sent = jnp.zeros_like(lane)
+    seen = jnp.zeros_like(lane)
+    peers = jnp.zeros_like(lane)
+    theirs = jnp.zeros_like(lane)
+    for face, (peer, their, flip) in enumerate(faces):
+        match = target == peer
+        sent = jnp.where(match & (seen == slot), 2 * face + flip, sent)
+        seen = jnp.where(match, seen + 1, seen)
+        peers = jnp.where(number == face, peer, peers)
+        theirs = jnp.where(number == face, their, theirs)
+    place = jnp.zeros_like(lane)
+    for peer, their, _ in faces:
+        place = jnp.where((peers == peer) & (theirs > their), place + 1, place)
+    source = jnp.where(peers < 0, 0, peers)
+    place = jnp.where(peers < 0, 2, place)
+    return jnp.where(lane < 2 * blks, sent, jnp.where(lane < 2 * blks + FACES, source, place))
+
+
+def permuted(value, order):
+    return jnp.take_along_axis(value, order, axis=1, mode="promise_in_bounds")
 
 
 def split(value):
@@ -48,10 +60,10 @@
 
 def kernel(
     blks, lines,
-    codes, viscous, advection, state, inverse, out,
-    points, inv, weight_k, weight_j, weight_i, own, table, slots, arrived,
+    links, viscous, advection, state, inverse, out,
+    points, inv, weight_k, weight_j, weight_i, codes_out, codes, table, slots, arrived,
     rim_out, rim_in, halo_j, halo_k, turned, sent, lines_in, result,
-    load_sem, inv_sem, rim_send, rim_recv, face_send, face_recv, line_send, line_recv, out_sem,
+    load_sem, inv_sem, codes_sem, rim_send, rim_recv, face_send, face_recv, line_send, line_recv, out_sem,
 ):
     me = lax.axis_index("blk")
     row = lax.axis_index("line")
@@ -85,81 +97,83 @@
     lax.fori_loop(1, blks, greet_blk, 0)
     lax.fori_loop(1, lines, greet_line, 0)
 
+    codes_out[...] = link_codes(links, NB, blks)
+    codes_copy = pltpu.make_async_copy(codes_out, codes, codes_sem)
+    codes_copy.start()
+
     lane = lax.broadcasted_iota(jnp.int32, (ROWS, 128), 1)
     level = lax.broadcasted_iota(jnp.int32, (ROWS, 128), 0)
     left = lane < 64
     even = (lane & 1) == 0
+    point = lane & 63
 
     pltpu.make_async_copy(points, points, load_sem).wait()
 
-    def take_rims(unit, carry):
-        rim_out[0, unit] = points[unit, pl.ds(0, PAIRS, stride=ROWS), :]
-        rim_out[1, unit] = points[unit, pl.ds(ROWS - 1, PAIRS, stride=ROWS), :]
-        return carry
-
-    lax.fori_loop(0, NU, take_rims, 0)
-
-    def merged(values):
-        count = 1
-        shift = (lane + 1) & 63
-        while values.shape[0] > 1:
-            pairs = values.reshape(values.shape[0] // 2, 2, ROWS, 128)
-            moved = pltpu.roll(pairs[:, 1], 2 * count, axis=2)
-            values = jnp.where((shift < 2 * count)[None], pairs[:, 0], moved)
-            count *= 2
-        return values[0]
-
-    def take_faces(unit, carry):
-        block, field = unit // NF, lax.rem(unit, NF)
-        cells = points[unit].reshape(PAIRS, ROWS, 128)
-        own[2 * block, field] = jnp.where(left, cells[0], cells[PAIRS - 1])
-        mixed = merged(cells)
-        low = jnp.where(even, mixed, pltpu.roll(mixed, 65, axis=1))
-        high = jnp.where(even, pltpu.roll(mixed, 1, axis=1), pltpu.roll(mixed, 66, axis=1))
-        own[2 * block + 1, field] = jnp.where(left, low, high)
-        return carry
-
-    lax.fori_loop(0, NU, take_faces, 0)
-
-    def fill_table(item, carry):
-        pair, field = item // NF, lax.rem(item, NF)
-        forward = own[pair, field]
-        backward = forward
-        for bit in (1, 2, 4, 8, 16, 32):
-            backward = jnp.where(
-                (lane & bit) != 0,
-                pltpu.roll(backward, bit, axis=1),
-                pltpu.roll(backward, 128 - bit, axis=1),
-            )
-        for flip, value in ((0, forward), (1, backward)):
-            other = pltpu.roll(value, 64, axis=1)
-            table[4 * pair + flip, field] = jnp.where(left, value, other)
-            table[4 * pair + 2 + flip, field] = jnp.where(left, other, value)
-        return carry
-
-    lax.fori_loop(0, 2 * NB * NF, fill_table, 0)
+    def take_rims(block, carry):
+        for field in range(NF):
+            unit = block * NF + field
+            rim_out[0, unit] = points[unit, pl.ds(0, PAIRS, stride=ROWS), :]
+            rim_out[1, unit] = points[unit, pl.ds(ROWS - 1, PAIRS, stride=ROWS), :]
+        return carry
+
+    lax.fori_loop(0, NB, take_rims, 0)
+
+    key = ((lane + 1) & 63) >> 1
+    bits = [((key >> bit) & 1) == 1 for bit in range(5)]
+
+    def mixed_low(where):
+        return (where & 1) * 64 + (where & 62)
+
+    low_order = [mixed_low(point), mixed_low(63 - point)]
+    k_orders = low_order + [(order + 63) & 127 for order in low_order]
+    j_orders = [point, 63 - point, 64 + point, 127 - point]
+
+    def take_faces(block, carry):
+        for field in range(NF):
+            unit = block * NF + field
+            cells = [points[unit, pl.ds(pair * ROWS, ROWS), :] for pair in range(PAIRS)]
+            j_faces = jnp.where(left, cells[0], cells[PAIRS - 1])
+            tiles = [pltpu.roll(cell, 2 * pair, axis=1) for pair, cell in enumerate(cells)]
+            for bit in bits:
+                tiles = [
+                    jnp.where(bit, high, low) for low, high in zip(tiles[::2], tiles[1::2])
+                ]
+            for number, order in enumerate(j_orders):
+                table[8 * block + number, field] = permuted(j_faces, order)
+            for number, order in enumerate(k_orders):
+                table[8 * block + 4 + number, field] = permuted(tiles[0], order)
+        return carry
+
+    lax.fori_loop(0, NB, take_faces, 0)
+    codes_copy.wait()
+
+    def fill_slots(target, carry):
+        slots[target] = jnp.where(
+            left[None], table[codes[0, 2 * target]], table[codes[0, 2 * target + 1]]
+        )
+        return carry
+
+    lax.fori_loop(0, blks, fill_slots, 0)
 
     pl.semaphore_wait(barrier, blks + lines - 2)
 
-    rims = [
-        pltpu.make_async_remote_copy(
-            src_ref=rim_out.at[side],
-            dst_ref=rim_in.at[1 - side],
-            send_sem=rim_send.at[side],
-            recv_sem=rim_recv.at[1 - side],
+    def rim_copy(block, side):
+        rows = pl.ds(block * NF, NF)
+        return pltpu.make_async_remote_copy(
+            src_ref=rim_out.at[side, rows],
+            dst_ref=rim_in.at[1 - side, rows],
+            send_sem=rim_send.at[side, block],
+            recv_sem=rim_recv.at[1 - side, block],
             device_id=(me, lax.rem(row + (lines - 1 if side == 0 else 1), lines)),
             device_id_type=MESH,
         )
-        for side in (0, 1)
-    ]
-    for rim in rims:
-        rim.start()
+
+    for block in range(NB):
+        for side in (0, 1):
+            rim_copy(block, side).start()
 
     def send_faces(step, carry):
         target = lax.rem(me + step, blks)
-        slots[target] = jnp.where(
-            left[None], table[codes[2 * target]], table[codes[2 * target + 1]]
-        )
         pltpu.make_async_remote_copy(
             src_ref=slots.at[target],
             dst_ref=arrived.at[me],
@@ -211,8 +225,6 @@
 
     lax.fori_loop(0, NU, make_weights, 0)
 
-    for rim in rims:
-        rim.wait()
     pltpu.make_async_copy(
         slots.at[pl.ds(0, blks - 1)], slots.at[pl.ds(0, blks - 1)], face_send
     ).wait()
@@ -223,22 +235,22 @@
     whole = (NF, ROWS, 128)
 
     def facing(face, half):
-        source, slot = codes[2 * blks + face], codes[2 * blks + FACES + face]
+        source = codes[0, 2 * blks + face]
+        slots_of = jnp.full(whole, codes[0, 2 * blks + FACES + face], jnp.int32)
         value = arrived[source]
-        slots_of = jnp.full(whole, slot, jnp.int32)
         value = jnp.where(slots_of == half, value, pltpu.roll(value, 64, axis=2))
-        return jnp.where(slots_of == 2, own[face // 2], value)
-
+        return jnp.where(slots_of == 2, table[2 * face], value)
+
+    mixed = jnp.where(even, lane, (lane + 65) & 127)
+    back_order = jnp.where(mixed < 64, mixed, mixed - 63) + jnp.where(even, 0, 64)
     for pair in range(2 * NB):
         value = jnp.where(left[None], facing(2 * pair, 0), facing(2 * pair + 1, 1))
-        block = pair // 2
-        if pair % 2 == 0:
-            halo_j[pl.ds(block * NF, NF)] = value
-        else:
-            far = jnp.where(left[None], value, pltpu.roll(value, 63, axis=2))
-            ahead = ((lane >= 63) & (lane < 126))[None]
-            near = jnp.where(ahead, pltpu.roll(value, 127, axis=2), pltpu.roll(value, 62, axis=2))
-            halo_k[pl.ds(block * NF, NF)] = jnp.where(even[None], far, near)
+        for field in range(NF):
+            unit = pair // 2 * NF + field
+            if pair % 2 == 0:
+                halo_j[unit] = value[field]
+            else:
+                halo_k[unit] = permuted(value[field], back_order)
 
     first = jnp.full((ROWS, 128), row, jnp.int32) == 0
     last = jnp.full((ROWS, 128), row, jnp.int32) == lines - 1
@@ -259,11 +271,17 @@
 
     def sweep_jk(unit, carry):
         block, field = unit // NF, lax.rem(unit, NF)
+
+        @pl.when(field == 0)
+        def _():
+            for side in (0, 1):
+                rim_copy(block, side).wait_recv()
+
         ahead, behind = [], []
         middle = jnp.float32(0.0)
         for direction in range(3):
-            diffuse = viscous[block, direction, field]
-            half_speed = 0.5 * advection[block, direction, field]
+            diffuse = viscous[direction, block, field]
+            half_speed = 0.5 * advection[direction, block, field]
             ahead.append(diffuse - half_speed)
             behind.append(diffuse + half_speed)
             middle = middle - 2.0 * diffuse
@@ -354,20 +372,23 @@
         return carry
 
     lax.fori_loop(0, NU, finish, 0)
+    for block in range(NB):
+        for side in (0, 1):
+            rim_copy(block, side).wait_send()
     pltpu.make_async_copy(result, out, out_sem).wait()
 
 
 def on_device(state, viscous, advection, sweep_inverse, face_links):
     blks, lines = lax.axis_size("blk"), lax.axis_size("line")
     blocks_here, fields, rows_here, plane = state.shape
-    codes = link_codes(face_links, blocks_here, blks)
     smem = pl.BlockSpec(memory_space=pltpu.SMEM)
     anywhere = pl.BlockSpec(memory_space=pl.ANY)
+    far = pl.BlockSpec(memory_space=pltpu.HBM)
     dma = pltpu.SemaphoreType.DMA
     out = pl.pallas_call(
         functools.partial(kernel, blks, lines),
         out_shape=jax.ShapeDtypeStruct((NU, NL, plane // lines), F32),
-        in_specs=[smem, smem, smem, anywhere, anywhere],
+        in_specs=[smem, smem, smem, far, far],
         out_specs=anywhere,
         scratch_shapes=[
             pltpu.VMEM((NU, PAIRS * ROWS, 128), F32),
@@ -375,7 +396,8 @@
             pltpu.VMEM((NU, 256, 128), BF16),
             pltpu.VMEM((NU, NL, 128), BF16),
             pltpu.VMEM((NU, NL, 128), BF16),
-            pltpu.VMEM((2 * NB, NF, ROWS, 128), F32),
+            pltpu.VMEM((8, CODES), jnp.int32),
+            pltpu.SMEM((8, CODES), jnp.int32),
             pltpu.VMEM((2 * FACES, NF, ROWS, 128), F32),
             pltpu.VMEM((blks, NF, ROWS, 128), F32),
             pltpu.VMEM((blks, NF, ROWS, 128), F32),
@@ -387,16 +409,16 @@
             pltpu.VMEM((NU, PAIRS * ROWS, 128), F32),
             pltpu.VMEM((NU, lines, PAIRS, 128), F32),
             pltpu.VMEM((NU, NL, plane // lines), F32),
-            dma, dma, dma((2,)), dma((2,)), dma, dma, dma((NU,)), dma((NU,)), dma,
+            dma, dma, dma, dma((2, NB)), dma((2, NB)), dma, dma, dma((NU,)), dma((NU,)), dma,
         ],
         compiler_params=pltpu.CompilerParams(
-            collective_id=0, has_side_effects=True, vmem_limit_bytes=40 * 1024 * 1024
+            collective_id=0, has_side_effects=True, vmem_limit_bytes=63 * 1024 * 1024
         ),
         name="implicit_update",
     )(
-        codes,
-        viscous,
-        advection,
+        face_links.transpose(2, 0, 1),
+        viscous.transpose(1, 0, 2),
+        advection.transpose(1, 0, 2),
         state.reshape(NU, rows_here, plane),
         sweep_inverse.reshape(3 * NU, NL, NL),
     )

time: 113 us -> 85.4 us (0.76)
  Pallas kernels: 105 us -> 81.3 us
  local copies, waits for them, and re-layouts: 6.94 us -> 3.57 us
    pallas_call x1, Pallas kernels: 105 us -> 81.3 us  [on_device(): pl.pallas_call(functools.partial(kernel, blks, lines), out_shape=jax.Shap...]
    unnamed x7 -> x1, local copies, waits for them, and re-layouts: 6.17 us -> 3.57 us
where the time goes in v1:
time: 85.4 us; the launch traced here: 84.8 us
  Pallas kernels  81.3 us (95%)
  local copies, waits for them, and re-layouts  3.57 us (4%)
    pallas_call x1, Pallas kernels, on_device(): pl.pallas_call(functools.partial(kernel, blks, lines), out_shape=jax.Shap...  81.3 us
    unnamed x1, local copies, waits for them, and re-layouts  3.57 us

profile of v1, /device:TPU:1, one launch (start us, length us, event | category | flops | bytes accessed | tf_op | source)
XLA Modules:
  0.0 84.8 jit_solution(7390158454419956102)
XLA Ops:
  0.0 81.3 %implicit_update.1 = f32[20,64,512]{2,1,0:T(8,128)} custom-call(s32[3,4,4]{2,1,0:T(4,128)} %bitcast.9, f32[3,4,5]{2,1,0:T(4,128)} %bitcast.10, f32[3,4,5]{2,1,0:T(4,128)} %bitcast.11, f32[20,8,4096]{2,1,0:T(8,128)} %bitcast.7, f32[60,64,64]{2,1,0:T(8,128)} %bitcast.8), custom_call_target="tpu_custom_call" | custom-call | tf_op jit(solution)/shard_map/implicit_update/pallas_call | solution.py:388
  81.3 3.6 %copy.7 = f32[4,5,64,512]{3,2,1,0:T(8,128)} copy(f32[4,5,64,512]{3,2,1,0:T(8,128)} %bitcast.6) | data formatting | bytes 5242880

commit v2 on v1

--- a/solution.py
+++ b/solution.py
@@ -19,6 +19,7 @@
 PAIRS = 32
 FACES = 4 * NB
 CODES = 128
+GROUPS = ((0, 1), (1, 2), (3, 2))
 
 
 def link_codes(links, blocks_here, blks):
@@ -82,20 +83,19 @@
 
     barrier = pltpu.get_barrier_semaphore()
 
-    def greet_blk(step, carry):
-        pl.semaphore_signal(
-            barrier, inc=1, device_id=(lax.rem(me + step, blks), row), device_id_type=MESH
-        )
-        return carry
-
-    def greet_line(step, carry):
-        pl.semaphore_signal(
-            barrier, inc=1, device_id=(me, lax.rem(row + step, lines)), device_id_type=MESH
-        )
-        return carry
-
-    lax.fori_loop(1, blks, greet_blk, 0)
-    lax.fori_loop(1, lines, greet_line, 0)
+    def greet(target, line):
+        pl.semaphore_signal(barrier, inc=1, device_id=(target, line), device_id_type=MESH)
+
+    side = 4
+    mine = (me // (2 * side), lax.rem(me // 2, side), lax.rem(me, 2))
+    away = [(y, x, core) for y in range(side) for x in range(side) for core in range(2)]
+    away.sort(key=lambda step: -min(step[0], side - step[0]) - min(step[1], side - step[1]))
+    for step in sorted(range(1, lines), key=lambda step: -min(step, lines - step)):
+        greet(me, lax.rem(row + step, lines))
+    for y, x, core in away:
+        if y or x or core:
+            ring_y, ring_x = lax.rem(mine[0] + y, side), lax.rem(mine[1] + x, side)
+            greet((ring_y * side + ring_x) * 2 + lax.rem(mine[2] + core, 2), row)
 
     codes_out[...] = link_codes(links, NB, blks)
     codes_copy = pltpu.make_async_copy(codes_out, codes, codes_sem)
@@ -112,8 +112,8 @@
     def take_rims(block, carry):
         for field in range(NF):
             unit = block * NF + field
-            rim_out[0, unit] = points[unit, pl.ds(0, PAIRS, stride=ROWS), :]
-            rim_out[1, unit] = points[unit, pl.ds(ROWS - 1, PAIRS, stride=ROWS), :]
+            rim_out[0, field, block] = points[unit, pl.ds(0, PAIRS, stride=ROWS), :]
+            rim_out[1, field, block] = points[unit, pl.ds(ROWS - 1, PAIRS, stride=ROWS), :]
         return carry
 
     lax.fori_loop(0, NB, take_rims, 0)
@@ -157,34 +157,38 @@
 
     pl.semaphore_wait(barrier, blks + lines - 2)
 
-    def rim_copy(block, side):
-        rows = pl.ds(block * NF, NF)
+    def rim_copy(group, side):
+        fields = pl.ds(*GROUPS[group])
         return pltpu.make_async_remote_copy(
-            src_ref=rim_out.at[side, rows],
-            dst_ref=rim_in.at[1 - side, rows],
-            send_sem=rim_send.at[side, block],
-            recv_sem=rim_recv.at[1 - side, block],
+            src_ref=rim_out.at[side, fields],
+            dst_ref=rim_in.at[1 - side, fields],
+            send_sem=rim_send.at[side, group],
+            recv_sem=rim_recv.at[1 - side, group],
             device_id=(me, lax.rem(row + (lines - 1 if side == 0 else 1), lines)),
             device_id_type=MESH,
         )
 
-    for block in range(NB):
+    for group, (field, fields) in enumerate(GROUPS):
         for side in (0, 1):
-            rim_copy(block, side).start()
-
-    def send_faces(step, carry):
-        target = lax.rem(me + step, blks)
-        pltpu.make_async_remote_copy(
-            src_ref=slots.at[target],
-            dst_ref=arrived.at[me],
-            send_sem=face_send,
-            recv_sem=face_recv,
-            device_id=(target, row),
-            device_id_type=MESH,
-        ).start()
-        return carry
-
-    lax.fori_loop(1, blks, send_faces, 0)
+            rim_copy(group, side).start()
+
+        def send_faces(step, carry):
+            target = lax.rem(me + step, blks)
+            pltpu.make_async_remote_copy(
+                src_ref=slots.at[target, pl.ds(field, fields)],
+                dst_ref=arrived[group].at[me],
+                send_sem=face_send.at[group],
+                recv_sem=face_recv.at[group],
+                device_id=(target, row),
+                device_id_type=MESH,
+            ).start()
+            return carry
+
+        lax.fori_loop(1, blks, send_faces, 0)
+
+    def all_faces(group, sems):
+        part = arrived[group].at[pl.ds(0, blks - 1)]
+        return pltpu.make_async_copy(part, part, sems.at[group])
 
     inv_copy.wait()
     deep = lax.broadcasted_iota(jnp.int32, (NL, 128), 0)
@@ -225,32 +229,30 @@
 
     lax.fori_loop(0, NU, make_weights, 0)
 
-    pltpu.make_async_copy(
-        slots.at[pl.ds(0, blks - 1)], slots.at[pl.ds(0, blks - 1)], face_send
-    ).wait()
-    pltpu.make_async_copy(
-        arrived.at[pl.ds(0, blks - 1)], arrived.at[pl.ds(0, blks - 1)], face_recv
-    ).wait()
-
-    whole = (NF, ROWS, 128)
-
-    def facing(face, half):
-        source = codes[0, 2 * blks + face]
-        slots_of = jnp.full(whole, codes[0, 2 * blks + FACES + face], jnp.int32)
-        value = arrived[source]
-        value = jnp.where(slots_of == half, value, pltpu.roll(value, 64, axis=2))
-        return jnp.where(slots_of == 2, table[2 * face], value)
-
     mixed = jnp.where(even, lane, (lane + 65) & 127)
     back_order = jnp.where(mixed < 64, mixed, mixed - 63) + jnp.where(even, 0, 64)
-    for pair in range(2 * NB):
-        value = jnp.where(left[None], facing(2 * pair, 0), facing(2 * pair + 1, 1))
-        for field in range(NF):
-            unit = pair // 2 * NF + field
-            if pair % 2 == 0:
-                halo_j[unit] = value[field]
-            else:
-                halo_k[unit] = permuted(value[field], back_order)
+
+    def facing(face, half, group, field):
+        source = codes[0, 2 * blks + face]
+        slots_of = jnp.full((ROWS, 128), codes[0, 2 * blks + FACES + face], jnp.int32)
+        value = arrived[group][source, field - GROUPS[group][0]]
+        value = jnp.where(slots_of == half, value, pltpu.roll(value, 64, axis=1))
+        return jnp.where(slots_of == 2, table[2 * face, field], value)
+
+    def take_halos(group):
+        for side in (0, 1):
+            rim_copy(group, side).wait_recv()
+        all_faces(group, face_recv).wait()
+        for field in range(GROUPS[group][0], sum(GROUPS[group])):
+            for pair in range(2 * NB):
+                low = facing(2 * pair, 0, group, field)
+                high = facing(2 * pair + 1, 1, group, field)
+                value = jnp.where(left, low, high)
+                unit = pair // 2 * NF + field
+                if pair % 2 == 0:
+                    halo_j[unit] = value
+                else:
+                    halo_k[unit] = permuted(value, back_order)
 
     first = jnp.full((ROWS, 128), row, jnp.int32) == 0
     last = jnp.full((ROWS, 128), row, jnp.int32) == lines - 1
@@ -269,14 +271,14 @@
             device_id_type=MESH,
         )
 
-    def sweep_jk(unit, carry):
-        block, field = unit // NF, lax.rem(unit, NF)
-
-        @pl.when(field == 0)
-        def _():
-            for side in (0, 1):
-                rim_copy(block, side).wait_recv()
-
+    def unit_of(turn):
+        field, block = turn // NB, lax.rem(turn, NB)
+        return field, block, block * NF + field
+
+    def sweep_jk(turn, carry):
+        field, block, unit = unit_of(turn)
+        for group in range(len(GROUPS)):
+            pl.when(turn == NB * GROUPS[group][0])(functools.partial(take_halos, group))
         ahead, behind = [], []
         middle = jnp.float32(0.0)
         for direction in range(3):
@@ -291,8 +293,8 @@
         summed = []
         for pair in range(PAIRS):
             cell, turn = cells[pair], turns[pair]
-            below = jnp.broadcast_to(rim_in[0, unit, pl.ds(pair, 1), :], (ROWS, 128))
-            above = jnp.broadcast_to(rim_in[1, unit, pl.ds(pair, 1), :], (ROWS, 128))
+            below = jnp.broadcast_to(rim_in[0, field, block, pl.ds(pair, 1), :], (ROWS, 128))
+            above = jnp.broadcast_to(rim_in[1, field, block, pl.ds(pair, 1), :], (ROWS, 128))
             below = jnp.where(first, cell, below)
             above = jnp.where(last, cell, above)
             i_minus = jnp.where(top, below, pltpu.roll(cell, 1, axis=0))
@@ -351,7 +353,8 @@
 
     others = pl.ds(0, lines - 1)
 
-    def sweep_i(unit, carry):
+    def sweep_i(turn, carry):
+        unit = unit_of(turn)[2]
         pltpu.make_async_copy(
             lines_in.at[unit, others], lines_in.at[unit, others], line_recv.at[unit]
         ).wait()
@@ -372,9 +375,10 @@
         return carry
 
     lax.fori_loop(0, NU, finish, 0)
-    for block in range(NB):
+    for group in range(len(GROUPS)):
+        all_faces(group, face_send).wait()
         for side in (0, 1):
-            rim_copy(block, side).wait_send()
+            rim_copy(group, side).wait_send()
     pltpu.make_async_copy(result, out, out_sem).wait()
 
 
@@ -385,9 +389,10 @@
     anywhere = pl.BlockSpec(memory_space=pl.ANY)
     far = pl.BlockSpec(memory_space=pltpu.HBM)
     dma = pltpu.SemaphoreType.DMA
+    parts = len(GROUPS)
     out = pl.pallas_call(
         functools.partial(kernel, blks, lines),
-        out_shape=jax.ShapeDtypeStruct((NU, NL, plane // lines), F32),
+        out_shape=pltpu.VMEM((NU, NL, plane // lines), F32),
         in_specs=[smem, smem, smem, far, far],
         out_specs=anywhere,
         scratch_shapes=[
@@ -400,19 +405,19 @@
             pltpu.SMEM((8, CODES), jnp.int32),
             pltpu.VMEM((2 * FACES, NF, ROWS, 128), F32),
             pltpu.VMEM((blks, NF, ROWS, 128), F32),
-            pltpu.VMEM((blks, NF, ROWS, 128), F32),
-            pltpu.VMEM((2, NU, PAIRS, 128), F32),
-            pltpu.VMEM((2, NU, PAIRS, 128), F32),
+            [pltpu.VMEM((blks, fields, ROWS, 128), F32) for _, fields in GROUPS],
+            pltpu.VMEM((2, NF, NB, PAIRS, 128), F32),
+            pltpu.VMEM((2, NF, NB, PAIRS, 128), F32),
             pltpu.VMEM((NU, ROWS, 128), F32),
             pltpu.VMEM((NU, ROWS, 128), F32),
             pltpu.VMEM((PAIRS * ROWS, 128), F32),
             pltpu.VMEM((NU, PAIRS * ROWS, 128), F32),
             pltpu.VMEM((NU, lines, PAIRS, 128), F32),
             pltpu.VMEM((NU, NL, plane // lines), F32),
-            dma, dma, dma, dma((2, NB)), dma((2, NB)), dma, dma, dma((NU,)), dma((NU,)), dma,
+            dma, dma, dma, dma((2, parts)), dma((2, parts)), dma((parts,)), dma((parts,)), dma((NU,)), dma((NU,)), dma,
         ],
         compiler_params=pltpu.CompilerParams(
-            collective_id=0, has_side_effects=True, vmem_limit_bytes=63 * 1024 * 1024
+            collective_id=0, has_side_effects=True, vmem_limit_bytes=60 * 1024 * 1024
         ),
         name="implicit_update",
     )(

time: 85.4 us -> 80 us (0.937)
  Pallas kernels: 81.3 us -> 78.4 us
  local copies, waits for them, and re-layouts: 3.57 us -> 1.49 us
    pallas_call x1, Pallas kernels: 81.3 us -> 78.4 us  [on_device(): pl.pallas_call(functools.partial(kernel, blks, lines), out_shape=pltpu.VM...]
    unnamed x1, local copies, waits for them, and re-layouts: 3.57 us -> 1.49 us
where the time goes in v2:
time: 80 us; the launch traced here: 79.9 us
  Pallas kernels  78.4 us (98%)
  local copies, waits for them, and re-layouts  1.49 us (2%)
    pallas_call x1, Pallas kernels, on_device(): pl.pallas_call(functools.partial(kernel, blks, lines), out_shape=pltpu.VM...  78.4 us

profile of v2, /device:TPU:1, one launch (start us, length us, event | category | flops | bytes accessed | tf_op | source)
XLA Modules:
  0.0 79.9 jit_solution(5226449777762231725)
XLA Ops:
  0.0 78.4 %implicit_update.1 = f32[20,64,512]{2,1,0:T(8,128)S(1)} custom-call(s32[3,4,4]{2,1,0:T(4,128)} %bitcast.9, f32[3,4,5]{2,1,0:T(4,128)} %bitcast.10, f32[3,4,5]{2,1,0:T(4,128)} %bitcast.11, f32[20,8,4096]{2,1,0:T(8,128)} %bitcast.7, f32[60,64,64]{2,1,0:T(8,128)} %bitcast.8), custom_call_target="tpu_custom_call" | custom-call | tf_op jit(solution)/shard_map/implicit_update/pallas_call | solution.py:393
  78.4 1.5 %copy.7 = f32[4,5,64,512]{3,2,1,0:T(8,128)} copy(f32[4,5,64,512]{3,2,1,0:T(8,128)S(1)} %bitcast.6) | data formatting | bytes 5242880

commit v3 on v2

--- a/solution.py
+++ b/solution.py
@@ -61,10 +61,11 @@
 
 def kernel(
     blks, lines,
-    links, viscous, advection, state, inverse, out,
+    links_far, viscous_far, advection_far, state, inverse, out,
+    links, viscous, advection,
     points, inv, weight_k, weight_j, weight_i, codes_out, codes, table, slots, arrived,
-    rim_out, rim_in, halo_j, halo_k, turned, sent, lines_in, result,
-    load_sem, inv_sem, codes_sem, rim_send, rim_recv, face_send, face_recv, line_send, line_recv, out_sem,
+    rim_out, rim_in, halo_j, halo_k, turned, sent, lines_in,
+    small_sem, load_sem, inv_sem, codes_sem, rim_send, rim_recv, face_send, face_recv, line_send, line_recv,
 ):
     me = lax.axis_index("blk")
     row = lax.axis_index("line")
@@ -75,11 +76,6 @@
             points.at[:, pl.ds(pair * ROWS, ROWS), :],
             load_sem,
         )
-
-    for pair in range(PAIRS):
-        load(pair).start()
-    inv_copy = pltpu.make_async_copy(inverse, inv, inv_sem)
-    inv_copy.start()
 
     barrier = pltpu.get_barrier_semaphore()
 
@@ -97,6 +93,21 @@
             ring_y, ring_x = lax.rem(mine[0] + y, side), lax.rem(mine[1] + x, side)
             greet((ring_y * side + ring_x) * 2 + lax.rem(mine[2] + core, 2), row)
 
+    small = [
+        pltpu.make_async_copy(source, target, small_sem.at[number])
+        for number, (source, target) in enumerate(
+            ((links_far, links), (viscous_far, viscous), (advection_far, advection))
+        )
+    ]
+    for copy in small:
+        copy.start()
+    for pair in range(PAIRS):
+        load(pair).start()
+    inv_copy = pltpu.make_async_copy(inverse, inv, inv_sem)
+    inv_copy.start()
+
+    for copy in small:
+        copy.wait()
     codes_out[...] = link_codes(links, NB, blks)
     codes_copy = pltpu.make_async_copy(codes_out, codes, codes_sem)
     codes_copy.start()
@@ -362,8 +373,7 @@
         columns = [
             values[:, pair * ROWS : (pair + 1) * ROWS, :].reshape(NL, 128) for pair in range(4)
         ]
-        result[unit] = sweep(weight_i[unit], jnp.concatenate(columns, axis=1))
-        pltpu.make_async_copy(result.at[unit], out.at[unit], out_sem).start()
+        out[unit] = sweep(weight_i[unit], jnp.concatenate(columns, axis=1))
         return carry
 
     lax.fori_loop(0, NU, sweep_i, 0)
@@ -379,23 +389,23 @@
         all_faces(group, face_send).wait()
         for side in (0, 1):
             rim_copy(group, side).wait_send()
-    pltpu.make_async_copy(result, out, out_sem).wait()
 
 
 def on_device(state, viscous, advection, sweep_inverse, face_links):
     blks, lines = lax.axis_size("blk"), lax.axis_size("line")
     blocks_here, fields, rows_here, plane = state.shape
-    smem = pl.BlockSpec(memory_space=pltpu.SMEM)
-    anywhere = pl.BlockSpec(memory_space=pl.ANY)
     far = pl.BlockSpec(memory_space=pltpu.HBM)
     dma = pltpu.SemaphoreType.DMA
     parts = len(GROUPS)
     out = pl.pallas_call(
         functools.partial(kernel, blks, lines),
         out_shape=pltpu.VMEM((NU, NL, plane // lines), F32),
-        in_specs=[smem, smem, smem, far, far],
-        out_specs=anywhere,
+        in_specs=[far] * 5,
+        out_specs=pl.BlockSpec(memory_space=pltpu.VMEM),
         scratch_shapes=[
+            pltpu.SMEM((3, NB, 4), jnp.int32),
+            pltpu.SMEM((3, NB, NF), F32),
+            pltpu.SMEM((3, NB, NF), F32),
             pltpu.VMEM((NU, PAIRS * ROWS, 128), F32),
             pltpu.VMEM((3 * NU, NL, NL), F32),
             pltpu.VMEM((NU, 256, 128), BF16),
@@ -413,8 +423,7 @@
             pltpu.VMEM((PAIRS * ROWS, 128), F32),
             pltpu.VMEM((NU, PAIRS * ROWS, 128), F32),
             pltpu.VMEM((NU, lines, PAIRS, 128), F32),
-            pltpu.VMEM((NU, NL, plane // lines), F32),
-            dma, dma, dma, dma((2, parts)), dma((2, parts)), dma((parts,)), dma((parts,)), dma((NU,)), dma((NU,)), dma,
+            dma((3,)), dma, dma, dma, dma((2, parts)), dma((2, parts)), dma((parts,)), dma((parts,)), dma((NU,)), dma((NU,)),
         ],
         compiler_params=pltpu.CompilerParams(
             collective_id=0, has_side_effects=True, vmem_limit_bytes=60 * 1024 * 1024

time: 80 us -> 78.3 us (0.979)
  Pallas kernels: 78.4 us -> 76.7 us
    pallas_call x1, Pallas kernels: 78.4 us -> 76.7 us  [on_device(): pl.pallas_call(functools.partial(kernel, blks, lines), out_shape=pltpu.VM...]
where the time goes in v3:
time: 78.3 us; the launch traced here: 78.2 us
  Pallas kernels  76.7 us (98%)
  local copies, waits for them, and re-layouts  1.49 us (2%)
    pallas_call x1, Pallas kernels, on_device(): pl.pallas_call(functools.partial(kernel, blks, lines), out_shape=pltpu.VM...  76.7 us

profile of v3, /device:TPU:1, one launch (start us, length us, event | category | flops | bytes accessed | tf_op | source)
XLA Modules:
  0.0 78.2 jit_solution(16333560074959323372)
XLA Ops:
  0.0 76.7 %implicit_update.1 = f32[20,64,512]{2,1,0:T(8,128)S(1)} custom-call(s32[3,4,4]{2,1,0:T(4,128)} %bitcast.9, f32[3,4,5]{2,1,0:T(4,128)} %bitcast.10, f32[3,4,5]{2,1,0:T(4,128)} %bitcast.11, f32[20,8,4096]{2,1,0:T(8,128)} %bitcast.7, f32[60,64,64]{2,1,0:T(8,128)} %bitcast.8), custom_call_target="tpu_custom_call" | custom-call | tf_op jit(solution)/shard_map/implicit_update/pallas_call | solution.py:400
  76.7 1.5 %copy.7 = f32[4,5,64,512]{3,2,1,0:T(8,128)} copy(f32[4,5,64,512]{3,2,1,0:T(8,128)S(1)} %bitcast.6) | data formatting | bytes 5242880

commit v4 on v3

--- a/solution.py
+++ b/solution.py
@@ -168,6 +168,8 @@
 
     pl.semaphore_wait(barrier, blks + lines - 2)
 
+    inner = (row > 0, row < lines - 1)
+
     def rim_copy(group, side):
         fields = pl.ds(*GROUPS[group])
         return pltpu.make_async_remote_copy(
@@ -181,7 +183,7 @@
 
     for group, (field, fields) in enumerate(GROUPS):
         for side in (0, 1):
-            rim_copy(group, side).start()
+            pl.when(inner[side])(rim_copy(group, side).start)
 
         def send_faces(step, carry):
             target = lax.rem(me + step, blks)
@@ -252,7 +254,7 @@
 
     def take_halos(group):
         for side in (0, 1):
-            rim_copy(group, side).wait_recv()
+            pl.when(inner[1 - side])(rim_copy(group, side).wait_recv)
         all_faces(group, face_recv).wait()
         for field in range(GROUPS[group][0], sum(GROUPS[group])):
             for pair in range(2 * NB):
@@ -388,7 +390,7 @@
     for group in range(len(GROUPS)):
         all_faces(group, face_send).wait()
         for side in (0, 1):
-            rim_copy(group, side).wait_send()
+            pl.when(inner[side])(rim_copy(group, side).wait_send)
 
 
 def on_device(state, viscous, advection, sweep_inverse, face_links):

time: 78.3 us -> 78.3 us (level)
  no operation moved by 1% of the time
where the time goes in v4:
time: 78.3 us; the launch traced here: 78.2 us
  Pallas kernels  76.7 us (98%)
  local copies, waits for them, and re-layouts  1.49 us (2%)
    pallas_call x1, Pallas kernels, on_device(): pl.pallas_call(functools.partial(kernel, blks, lines), out_shape=pltpu.VM...  76.7 us

profile of v4, /device:TPU:1, one launch (start us, length us, event | category | flops | bytes accessed | tf_op | source)
XLA Modules:
  0.0 78.2 jit_solution(4360099227492930717)
XLA Ops:
  0.0 76.7 %implicit_update.1 = f32[20,64,512]{2,1,0:T(8,128)S(1)} custom-call(s32[3,4,4]{2,1,0:T(4,128)} %bitcast.9, f32[3,4,5]{2,1,0:T(4,128)} %bitcast.10, f32[3,4,5]{2,1,0:T(4,128)} %bitcast.11, f32[20,8,4096]{2,1,0:T(8,128)} %bitcast.7, f32[60,64,64]{2,1,0:T(8,128)} %bitcast.8), custom_call_target="tpu_custom_call" | custom-call | tf_op jit(solution)/shard_map/implicit_update/pallas_call | solution.py:402
  76.7 1.5 %copy.7 = f32[4,5,64,512]{3,2,1,0:T(8,128)} copy(f32[4,5,64,512]{3,2,1,0:T(8,128)S(1)} %bitcast.6) | data formatting | bytes 5242880
